TPU v7x, 512 devices: a whole 4x8x8 slice. The times are simulated.
512 devices in a mesh: dp: 32 (over x, y_hi, core), fsdp: 16 (over y_lo, z).
Axes of the slice: x: 4, y: 8 (y_hi: 4, y_lo: 2; y = y_hi * 2 + y_lo), z: 8, core: 2. Of those that a mesh axis runs over, the one named last changes fastest.
Arguments:
- hidden: bfloat16 [4, 2048, 16, 4096], P(None, 'dp', 'fsdp'), may hold values from -6 to 6
- frozen_query_rows: bfloat16 [4, 2048, 16, 2048], P(None, 'dp', 'fsdp'), may hold values from -10 to 10
- output_gradient: bfloat16 [4, 2048, 16, 2048], P(None, 'dp', 'fsdp'), may hold values from -6 to 6
- token_log_ratio: float32 [4, 2048, 16], P(None, 'dp', 'fsdp'), may hold values from -0.15625 to 0.15625
- lengths: int32 [4], replicated, may hold values from 1 to 32768, as said below
- response_win_probability: float32 [4], replicated, may hold values from 0.05 to 0.95
- cached_prompt_keys: bfloat16 [1024, 512], P('fsdp'), may hold values from -7.5 to 7.5
- cached_prompt_values: bfloat16 [1024, 512], P('fsdp'), may hold values from -6 to 6
- adapter_down_factor: bfloat16 [4096, 64], P('fsdp'), may hold values from -0.09375 to 0.09375
- adapter_up_factor: bfloat16 [64, 2048], P(None, 'fsdp'), may hold values from -0.125 to 0.125
- attention_norm_gain: bfloat16 [4096], P('fsdp'), may hold values from 0.5 to 1.5
Outputs:
- grad_down: float32 [4096, 64], P('fsdp')
- grad_up: float32 [64, 2048], P(None, 'fsdp')
- seq_ratio: float32 [4], replicated
Inputs may be any that keep to these rules, and one draw needn't show every extreme that they name: The lengths sum to 65472 and the longest is exactly 32768.
All inputs are finite; a program needn't handle non-finite values.
Results may differ from a plain program's by a relative error of at most 0.012.
Values may be sent and summed in bfloat16 or wider, within the bound.
A program may use at most 128 MiB of HBM per device.

v0:
```python
import math
import jax
import jax.numpy as jnp
from jax import lax
from jax.sharding import PartitionSpec as P

HEAD_SIZE = 128
QUERY_HEADS = 16
KEY_VALUE_HEADS = 4
target_scale = 1.0
norm_epsilon = 1e-05


def attend(query_vectors, cotangent, key_rows, value_rows):
    row_count = query_vectors.shape[0]
    queries_per_group = QUERY_HEADS // KEY_VALUE_HEADS
    score_scale = 1.0 / math.sqrt(HEAD_SIZE)
    pieces = []
    for shared_key_head in range(KEY_VALUE_HEADS):
        head_start = shared_key_head * queries_per_group * HEAD_SIZE
        head_stop = head_start + queries_per_group * HEAD_SIZE
        head_query = query_vectors[:, head_start:head_stop].reshape(
            row_count, queries_per_group, HEAD_SIZE
        )
        head_grad = cotangent[:, head_start:head_stop].reshape(
            row_count, queries_per_group, HEAD_SIZE
        )
        head_key = key_rows[:, shared_key_head * HEAD_SIZE : (shared_key_head + 1) * HEAD_SIZE]
        head_value = value_rows[:, shared_key_head * HEAD_SIZE : (shared_key_head + 1) * HEAD_SIZE]
        scores = (
            jnp.einsum("nhd,jd->nhj", head_query, head_key, preferred_element_type=jnp.float32)
            * score_scale
        )
        row_top = jnp.max(scores, axis=2, keepdims=True)
        exponent = jnp.exp(scores - row_top)
        row_total = jnp.sum(exponent, axis=2, keepdims=True)
        weights = exponent.astype(jnp.bfloat16)
        mixed_out = (
            jnp.einsum("nhj,jd->nhd", weights, head_value, preferred_element_type=jnp.float32)
            / row_total
        )
        inner_prod = jnp.sum(head_grad.astype(jnp.float32) * mixed_out, axis=2, keepdims=True)
        grad_prob = jnp.einsum(
            "nhd,jd->nhj", head_grad, head_value, preferred_element_type=jnp.float32
        )
        grad_score = (weights.astype(jnp.float32) / row_total * (grad_prob - inner_prod)).astype(
            jnp.bfloat16
        )
        query_gradient = (
            jnp.einsum("nhj,jd->nhd", grad_score, head_key, preferred_element_type=jnp.float32)
            * score_scale
        )
        pieces.append(query_gradient.reshape(row_count, queries_per_group * HEAD_SIZE))
    return jnp.concatenate(pieces, axis=1).astype(jnp.bfloat16)


def body(
    hidden,
    frozen_query_rows,
    output_gradient,
    token_log_ratio,
    lengths,
    response_win_probability,
    cached_prompt_keys,
    cached_prompt_values,
    adapter_down_factor,
    adapter_up_factor,
    attention_norm_gain,
):
    fsdp_count = lax.axis_size("fsdp")
    dp_index = lax.axis_index("dp")
    fsdp_index = lax.axis_index("fsdp")
    responses, per_device, single, feature_count = hidden.shape
    home_rows = responses * per_device
    local_rows = jnp.arange(per_device, dtype=jnp.int32)
    position = (dp_index * per_device + local_rows) * fsdp_count + fsdp_index
    is_valid = position[None, :] < lengths[:, None]
    partial_value = jnp.sum(jnp.where(is_valid, token_log_ratio[:, :, 0], 0.0), axis=1)
    seq_ratio = lax.psum(partial_value, ("dp", "fsdp"))
    weighting = 2.0 * (seq_ratio - target_scale * (response_win_probability - 0.5)) / responses
    down_full, up_full, gain_full = (
        lax.all_gather(adapter_down_factor, "fsdp", axis=0, tiled=True),
        lax.all_gather(adapter_up_factor, "fsdp", axis=1, tiled=True),
        lax.all_gather(attention_norm_gain, "fsdp", axis=0, tiled=True),
    )
    key_rows, value_rows = (
        lax.all_gather(cached_prompt_keys, "fsdp", axis=0, tiled=True),
        lax.all_gather(cached_prompt_values, "fsdp", axis=0, tiled=True),
    )
    widened = hidden.reshape(home_rows, feature_count).astype(jnp.float32)
    inverse = lax.rsqrt(jnp.mean(widened * widened, axis=1, keepdims=True) + norm_epsilon)
    normed_input = (widened * inverse * gain_full.astype(jnp.float32)).astype(jnp.bfloat16)
    lowrank_hidden = jnp.dot(normed_input, down_full, preferred_element_type=jnp.float32).astype(
        jnp.bfloat16
    )
    row_mask = is_valid.reshape(home_rows)
    row_coef = jnp.repeat(weighting, per_device)
    base_rows = frozen_query_rows.reshape(home_rows, -1)
    cotangent = jnp.where(
        row_mask[:, None],
        row_coef[:, None] * output_gradient.reshape(home_rows, -1).astype(jnp.float32),
        0.0,
    ).astype(jnp.bfloat16)
    query_vectors = (
        base_rows.astype(jnp.float32)
        + jnp.dot(lowrank_hidden, up_full, preferred_element_type=jnp.float32)
    ).astype(jnp.bfloat16)
    query_gradient = attend(query_vectors, cotangent, key_rows, value_rows)
    up_term = jnp.dot(lowrank_hidden.T, query_gradient, preferred_element_type=jnp.float32)
    gradient_lowrank = jnp.dot(
        query_gradient, up_full.T, preferred_element_type=jnp.float32
    ).astype(jnp.bfloat16)
    down_term = jnp.dot(normed_input.T, gradient_lowrank, preferred_element_type=jnp.float32)
    down_sum, up_sum = lax.psum((down_term, up_term), ("dp", "fsdp"))
    down_factor_part = adapter_down_factor.shape[0]
    up_factor_part = adapter_up_factor.shape[1]
    grad_down = lax.dynamic_slice_in_dim(
        down_sum, fsdp_index * down_factor_part, down_factor_part, 0
    )
    grad_up = lax.dynamic_slice_in_dim(up_sum, fsdp_index * up_factor_part, up_factor_part, 1)
    return (grad_down, grad_up, seq_ratio)


def solution(mesh):
    in_specs = (
        P(None, "dp", "fsdp", None),
        P(None, "dp", "fsdp", None),
        P(None, "dp", "fsdp", None),
        P(None, "dp", "fsdp"),
        P(),
        P(),
        P("fsdp", None),
        P("fsdp", None),
        P("fsdp", None),
        P(None, "fsdp"),
        P("fsdp"),
    )
    out_specs = (P("fsdp", None), P(None, "fsdp"), P())
    return jax.shard_map(body, mesh=mesh, in_specs=in_specs, out_specs=out_specs, check_vma=False)
```

profile of v0, /device:TPU:17, one launch (start us, length us, event | category | flops | bytes accessed | tf_op | source)
XLA Modules:
  0.0 574.0 jit_solution(2248930495816452318)
XLA Ops:
  7.2 0.7 all-gather.4.cloned.1.call-update
  7.9 0.0 all-gather.6.cloned.1.call-start
  8.0 0.7 all-gather.6.cloned.1.call-update
  8.7 0.0 all-reduce.3.cloned.1.call-start
  8.7 0.9 select_reduce_fusion
  9.6 105.0 %psum.21 = f32[4]{0:T(128)S(1)} all-reduce(f32[4]{0:T(128)S(1)} %get-tuple-element.5), channel_id=1, replica_groups=mesh['dp'=32,'fsdp'=16] {'dp','fsdp'}, use_global_device_ids=true, to_apply=%region_4.5 | all-reduce | flops 4 | bytes 32 | tf_op jit(solution)/shard_map/psum | solution.py:79
  114.6 0.1 lt.29
  114.6 0.7 reshape.122
  115.3 0.7 subtract_multiply_fusion
  116.0 0.1 broadcast_in_dim.20
  116.0 0.1 mul.107
  116.1 2.1 multiply_reduce_fusion
  118.2 0.1 rsqrt.12
  118.3 24.8 %all-gather = bf16[16,1,256]{2,1,0:T(2,128)(2,1)S(1)} all-gather(bf16[1,1,256]{2,1,0:T(2,128)(2,1)S(1)} %reshape.122), channel_id=1, replica_groups=mesh['dp'=32,'fsdp'=16] {'fsdp'}, dimensions={0}, use_global_device_ids=true | all-gather | bytes 8704 | tf_op jit(solution)/shard_map/all_gather | solution.py:84
  143.1 2.2 fusion.1
  145.4 0.3 fusion.12
  145.7 1.3 slice_bitcast_fusion.35
  147.0 1.7 reshape.117
  148.7 1.7 reshape.114
  150.5 1.7 reshape.111
  152.2 0.8 reshape.108
  152.9 24.4 %all_gather.17 = bf16[64,2048]{1,0:T(8,128)(2,1)S(1)} all-gather(bf16[64,128]{1,0:T(8,128)(2,1)S(1)} %copy-done.17), channel_id=1, replica_groups=mesh['dp'=32,'fsdp'=16] {'fsdp'}, dimensions={1}, use_global_device_ids=true | all-gather | bytes 278528 | tf_op jit(solution)/shard_map/all_gather | solution.py:83
  177.3 27.5 %all_gather.16 = bf16[4096,64]{0,1:T(8,128)(2,1)S(1)} all-gather(bf16[256,64]{0,1:T(8,128)(2,1)S(1)} %copy-done.16), channel_id=1, replica_groups=mesh['dp'=32,'fsdp'=16] {'fsdp'}, dimensions={0}, use_global_device_ids=true | all-gather | bytes 557056 | tf_op jit(solution)/shard_map/all_gather | solution.py:82
  204.8 0.8 convolution_convert_fusion.1
  205.6 0.5 fusion.10
  206.0 0.1 copy-done.14
  206.2 0.9 slice_bitcast_fusion.11
  207.1 1.7 multiply_reduce_fusion.4
  208.8 2.0 copy-done
  210.8 0.9 fusion.2
  211.7 0.1 copy.27
  211.9 3.0 fusion.39
  215.0 0.8 fusion.26
  215.7 0.7 copy.28
  216.4 1.9 multiply_reduce_fusion.1
  218.3 1.9 copy-done.1
  220.3 0.9 fusion.8
  221.2 0.8 copy.39
  222.0 3.1 fusion.30
  225.1 0.8 fusion.29
  225.9 0.7 copy.40
  226.6 1.8 multiply_reduce_fusion.2
  228.4 2.0 copy-done.2
  230.3 0.9 fusion.6
  231.3 0.8 copy.35
  232.1 3.1 fusion.33
  235.2 0.8 fusion.28
  235.9 0.7 copy.36
  236.6 1.8 multiply_reduce_fusion.3
  238.4 1.9 copy-done.3
  240.4 1.1 fusion.4
  241.5 0.8 copy.31
  242.3 3.1 fusion.36
  245.4 0.8 fusion.27
  246.2 0.7 copy.32
  246.9 4.8 fusion.21
  251.7 4.8 fusion.24
  256.5 4.8 fusion.23
  261.3 4.8 fusion.22
  266.2 3.6 fusion.25
  269.8 2.2 fusion.70
  272.0 292.6 %all-reduce.3.cloned.1.call-done = (f32[4096,64]{0,1:T(8,128)}, f32[64,2048]{1,0:T(8,128)}) async-done(((f32[4096,64]{0,1:T(8,128)}, f32[64,2048]{1,0:T(8,128)}), (f32[4096,64]{0,1:T(8,128)}, f32[64,2048]{1,0:T(8,128)})) %all-reduce.3.cloned.1.call-update) | async-done | bytes 1572880 | tf_op jit(solution)/shard_map/psum | solution.py:114
  564.6 1.5 constant_dynamic-slice_fusion.1
  566.1 1.4 constant_dynamic-slice_fusion
  (66 shorter events, 0.2 us)
Async XLA Ops:
  7.2 138.2 %copy-start.6 = (bf16[4,64,1,2048]{3,1,2,0:T(8,128)(2,1)S(1)}, bf16[4,64,1,2048]{3,1,2,0:T(8,128)(2,1)}, u32[]{:S(2)}) copy-start(bf16[4,64,1,2048]{3,1,2,0:T(8,128)(2,1)} %param.13) | copy-start | bytes 3145732
  7.2 199.9 %all-gather.4.cloned.1.call-start = ((), (), s32[]{:S(2)}) async-start(), calls=%async_computation | async-start | bytes 1114112 | tf_op jit(solution)/shard_map/all_gather | solution.py:87
  7.9 204.0 %all-gather.6.cloned.1.call-start = ((), (), s32[]{:S(2)}) async-start(), calls=%async_computation.1 | async-start | bytes 1114112 | tf_op jit(solution)/shard_map/all_gather | solution.py:88
  8.7 555.9 %all-reduce.3.cloned.1.call-start = ((), (), s32[]{:S(2)}) async-start(), calls=%async_computation.2 | async-start | bytes 3145728 | tf_op jit(solution)/shard_map/psum | solution.py:114
  114.6 3.7 copy-start.31
  145.3 7.6 %copy-start.17 = (bf16[64,128]{1,0:T(8,128)(2,1)S(1)}, bf16[64,128]{1,0:T(8,128)(2,1)}, u32[]{:S(2)}) copy-start(bf16[64,128]{1,0:T(8,128)(2,1)} %param.20) | copy-start | bytes 49156
  145.4 32.0 %copy-start.16 = (bf16[256,64]{0,1:T(8,128)(2,1)S(1)}, bf16[256,64]{0,1:T(8,128)(2,1)}, u32[]{:S(2)}) copy-start(bf16[256,64]{0,1:T(8,128)(2,1)} %param.19) | copy-start | bytes 98308
  145.7 59.9 %copy-start.5 = (bf16[4,64,1,2048]{3,1,2,0:T(8,128)(2,1)S(1)}, bf16[4,64,1,2048]{3,1,2,0:T(8,128)(2,1)}, u32[]{:S(2)}) copy-start(bf16[4,64,1,2048]{3,1,2,0:T(8,128)(2,1)} %param.12) | copy-start | bytes 3145732
  205.6 0.6 copy-start.14
  208.8 2.0 copy-start
  210.8 4.2 copy-start.10
  211.7 6.6 %copy-start.18 = (f32[256,4]{0,1:T(4,128)}, f32[256,4]{0,1:T(4,128)S(1)}, u32[]{:S(2)}) copy-start(f32[256,4]{0,1:T(4,128)S(1)} %fusion.2) | copy-start | bytes 12292
  216.4 5.6 copy-start.4
  218.3 1.9 copy-start.1
  221.2 0.8 copy-start.19
  222.0 3.1 copy-start.9
  222.0 3.1 copy-start.11
  228.4 2.0 copy-start.2
  231.3 0.8 copy-start.21
  232.1 3.1 copy-start.8
  232.1 3.1 copy-start.12
  238.4 1.9 copy-start.3
  241.5 0.8 copy-start.23
  242.3 3.1 copy-start.7
  242.3 3.1 copy-start.13
  246.9 4.8 copy-start.20
  246.9 4.8 copy-start.25
  251.7 4.8 copy-start.22
  251.7 4.8 copy-start.26
  256.5 4.8 copy-start.24
  256.5 4.8 copy-start.27
  266.2 3.7 copy-start.15
  266.2 3.7 copy-start.28
  266.2 3.7 copy-start.29
  266.2 3.7 copy-start.30
Sparse Core Ops, SparseCore 0:
  10.1 66.9 all-gather.3
  79.2 69.6 all-gather.5
  272.2 292.3 all-reduce.2
where the time goes:
time: 575 us; the launch traced here: 574 us
  waiting for transfers between devices  294 us (51%)
  blocking collectives  182 us (32%)
  matrix products  45.8 us (8%)
  local copies, waits for them, and re-layouts  25.3 us (4%)
  between operations  14.1 us (2%)
  other arithmetic  13.1 us (2%)
    psum x1, waiting for transfers between devices, body(): down_sum, up_sum = lax.psum((down_term, up_term), ('dp', 'fsdp'))  293 us
    psum x1, blocking collectives, body(): seq_ratio = lax.psum(partial_value, ('dp', 'fsdp'))  105 us
    all_gather x1, blocking collectives, body(): lax.all_gather(adapter_down_factor, 'fsdp', axis=0, tiled=True)  27.5 us
    all_gather x1, blocking collectives, body(): lax.all_gather(attention_norm_gain, 'fsdp', axis=0, tiled=True)  24.8 us
    all_gather x1, blocking collectives, body(): lax.all_gather(adapter_up_factor, 'fsdp', axis=1, tiled=True)  24.4 us
    dot_general x4, matrix products, attend(): jnp.einsum('nhj,jd->nhd', grad_score, head_key, preferred_element_type=jn...  19.2 us
    dot_general x4, matrix products, attend(): jnp.einsum('nhj,jd->nhd', weights, head_value, preferred_element_type=jnp...  12.3 us
  transfers between devices with their start and end apart: 3, of which 1 were waited for; matrix products, arithmetic and copies ran while one was open for 3% of the time, Pallas kernels for 0%

commit v1 on v0

--- a/solution.py
+++ b/solution.py
@@ -111,7 +111,7 @@
         query_gradient, up_full.T, preferred_element_type=jnp.float32
     ).astype(jnp.bfloat16)
     down_term = jnp.dot(normed_input.T, gradient_lowrank, preferred_element_type=jnp.float32)
-    down_sum, up_sum = lax.psum((down_term, up_term), ("dp", "fsdp"))
+    down_sum, up_sum = lax.psum(lax.psum((down_term, up_term), "dp"), "fsdp")
     down_factor_part = adapter_down_factor.shape[0]
     up_factor_part = adapter_up_factor.shape[1]
     grad_down = lax.dynamic_slice_in_dim(

time: 575 us -> 738 us (1.28)
  the two profiles are of different devices: /device:TPU:17 before, /device:TPU:2 now
where the time goes in v1:
time: 738 us
  waiting for transfers between devices  435 us (59%)
  blocking collectives  204 us (28%)
  matrix products  45.8 us (6%)
  local copies, waits for them, and re-layouts  25.2 us (3%)
  between operations  14.1 us (2%)
  other arithmetic  13.1 us (2%)
    psum x2, waiting for transfers between devices, body(): down_sum, up_sum = lax.psum(lax.psum((down_term, up_term), 'dp'), 'fsdp')  434 us
    psum x1, blocking collectives, body(): seq_ratio = lax.psum(partial_value, ('dp', 'fsdp'))  107 us
    all_gather x1, blocking collectives, body(): lax.all_gather(adapter_down_factor, 'fsdp', axis=0, tiled=True)  34 us
    all_gather x1, blocking collectives, body(): lax.all_gather(adapter_up_factor, 'fsdp', axis=1, tiled=True)  31.7 us
    all_gather x1, blocking collectives, body(): lax.all_gather(attention_norm_gain, 'fsdp', axis=0, tiled=True)  30.7 us
    dot_general x4, matrix products, attend(): jnp.einsum('nhj,jd->nhd', grad_score, head_key, preferred_element_type=jn...  19.2 us
  transfers between devices with their start and end apart: 4, of which 2 were waited for; matrix products, arithmetic and copies ran while one was open for 3% of the time, Pallas kernels for 0%

profile of v1, /device:TPU:2, one launch (start us, length us, event | category | flops | bytes accessed | tf_op | source)
XLA Modules:
  0.0 737.6 jit_solution(1639249956733935230)
XLA Ops:
  7.2 0.7 all-gather.4.cloned.1.call-update
  8.0 0.7 all-gather.6.cloned.1.call-update
  8.7 0.9 select_reduce_fusion
  9.6 107.3 %psum.35 = f32[4]{0:T(128)S(1)} all-reduce(f32[4]{0:T(128)S(1)} %get-tuple-element.7), channel_id=1, replica_groups=mesh['dp'=32,'fsdp'=16] {'dp','fsdp'}, use_global_device_ids=true, to_apply=%region_4.5 | all-reduce | flops 4 | bytes 32 | tf_op jit(solution)/shard_map/psum | solution.py:79
  116.9 0.1 lt.29
  117.0 0.7 reshape.122
  117.6 0.7 subtract_multiply_fusion
  118.3 0.1 broadcast_in_dim.20
  118.4 0.1 mul.107
  118.4 2.1 multiply_reduce_fusion
  120.5 0.1 rsqrt.12
  120.6 30.7 %all-gather = bf16[16,1,256]{2,1,0:T(2,128)(2,1)S(1)} all-gather(bf16[1,1,256]{2,1,0:T(2,128)(2,1)S(1)} %reshape.122), channel_id=1, replica_groups=mesh['dp'=32,'fsdp'=16] {'fsdp'}, dimensions={0}, use_global_device_ids=true | all-gather | bytes 8704 | tf_op jit(solution)/shard_map/all_gather | solution.py:84
  151.4 2.2 fusion.1
  153.7 0.3 fusion.12
  154.0 1.3 slice_bitcast_fusion.35
  155.3 1.7 reshape.117
  157.0 1.7 reshape.114
  158.8 1.7 reshape.111
  160.5 0.8 reshape.108
  161.2 31.7 %all_gather.17 = bf16[64,2048]{1,0:T(8,128)(2,1)S(1)} all-gather(bf16[64,128]{1,0:T(8,128)(2,1)S(1)} %copy-done.17), channel_id=1, replica_groups=mesh['dp'=32,'fsdp'=16] {'fsdp'}, dimensions={1}, use_global_device_ids=true | all-gather | bytes 278528 | tf_op jit(solution)/shard_map/all_gather | solution.py:83
  192.9 34.0 %all_gather.16 = bf16[4096,64]{0,1:T(8,128)(2,1)S(1)} all-gather(bf16[256,64]{0,1:T(8,128)(2,1)S(1)} %copy-done.16), channel_id=1, replica_groups=mesh['dp'=32,'fsdp'=16] {'fsdp'}, dimensions={0}, use_global_device_ids=true | all-gather | bytes 557056 | tf_op jit(solution)/shard_map/all_gather | solution.py:82
  226.9 0.8 convolution_convert_fusion.1
  227.7 0.5 fusion.10
  228.1 0.1 copy-done.14
  228.3 0.9 slice_bitcast_fusion.11
  229.2 1.7 multiply_reduce_fusion.4
  231.0 2.0 copy-done
  233.0 0.9 fusion.2
  233.9 0.1 copy.27
  234.1 3.0 fusion.39
  237.1 0.8 fusion.26
  237.9 0.7 copy.28
  238.6 1.9 multiply_reduce_fusion.1
  240.5 1.9 copy-done.1
  242.4 0.9 fusion.8
  243.3 0.8 copy.39
  244.1 3.1 fusion.30
  247.2 0.8 fusion.29
  248.0 0.7 copy.40
  248.7 1.8 multiply_reduce_fusion.2
  250.5 1.9 copy-done.2
  252.4 0.9 fusion.6
  253.4 0.8 copy.35
  254.2 3.1 fusion.33
  257.3 0.8 fusion.28
  258.1 0.7 copy.36
  258.7 1.8 multiply_reduce_fusion.3
  260.5 1.9 copy-done.3
  262.5 1.1 fusion.4
  263.6 0.8 copy.31
  264.4 3.1 fusion.36
  267.5 0.8 fusion.27
  268.3 0.7 copy.32
  269.0 4.8 fusion.21
  273.8 4.8 fusion.24
  278.6 4.8 fusion.23
  283.4 4.8 fusion.22
  288.3 3.6 fusion.25
  291.9 2.2 fusion.70
  294.1 0.0 all-reduce.7.cloned.1.call-start
  294.2 272.8 %all-reduce.5.cloned.1.call-done = (f32[4096,64]{0,1:T(8,128)}, f32[64,2048]{1,0:T(8,128)}) async-done(((f32[4096,64]{0,1:T(8,128)}, f32[64,2048]{1,0:T(8,128)}), (f32[4096,64]{0,1:T(8,128)}, f32[64,2048]{1,0:T(8,128)})) %all-reduce.5.cloned.1.call-update) | async-done | bytes 1572880 | tf_op jit(solution)/shard_map/psum | solution.py:114
  567.1 161.1 %all-reduce.7.cloned.1.call-done = (f32[4096,64]{0,1:T(8,128)}, f32[64,2048]{1,0:T(8,128)}) async-done(((f32[4096,64]{0,1:T(8,128)}, f32[64,2048]{1,0:T(8,128)}), (f32[4096,64]{0,1:T(8,128)}, f32[64,2048]{1,0:T(8,128)})) %all-reduce.7.cloned.1.call-update) | async-done | bytes 1572880 | tf_op jit(solution)/shard_map/psum | solution.py:114
  728.2 1.5 constant_dynamic-slice_fusion.1
  729.7 1.4 constant_dynamic-slice_fusion
  (69 shorter events, 0.3 us)
Async XLA Ops:
  7.2 146.5 %copy-start.6 = (bf16[4,64,1,2048]{3,1,2,0:T(8,128)(2,1)S(1)}, bf16[4,64,1,2048]{3,1,2,0:T(8,128)(2,1)}, u32[]{:S(2)}) copy-start(bf16[4,64,1,2048]{3,1,2,0:T(8,128)(2,1)} %param.13) | copy-start | bytes 3145732
  7.2 222.1 %all-gather.4.cloned.1.call-start = ((), (), s32[]{:S(2)}) async-start(), calls=%async_computation | async-start | bytes 1114112 | tf_op jit(solution)/shard_map/all_gather | solution.py:87
  7.9 226.1 %all-gather.6.cloned.1.call-start = ((), (), s32[]{:S(2)}) async-start(), calls=%async_computation.1 | async-start | bytes 1114112 | tf_op jit(solution)/shard_map/all_gather | solution.py:88
  8.7 558.4 %all-reduce.5.cloned.1.call-start = ((), (), s32[]{:S(2)}) async-start(), calls=%async_computation.2 | async-start | bytes 3145728 | tf_op jit(solution)/shard_map/psum | solution.py:114
  116.9 3.7 copy-start.31
  153.6 7.6 %copy-start.17 = (bf16[64,128]{1,0:T(8,128)(2,1)S(1)}, bf16[64,128]{1,0:T(8,128)(2,1)}, u32[]{:S(2)}) copy-start(bf16[64,128]{1,0:T(8,128)(2,1)} %param.20) | copy-start | bytes 49156
  153.7 39.3 %copy-start.16 = (bf16[256,64]{0,1:T(8,128)(2,1)S(1)}, bf16[256,64]{0,1:T(8,128)(2,1)}, u32[]{:S(2)}) copy-start(bf16[256,64]{0,1:T(8,128)(2,1)} %param.19) | copy-start | bytes 98308
  154.0 73.7 %copy-start.5 = (bf16[4,64,1,2048]{3,1,2,0:T(8,128)(2,1)S(1)}, bf16[4,64,1,2048]{3,1,2,0:T(8,128)(2,1)}, u32[]{:S(2)}) copy-start(bf16[4,64,1,2048]{3,1,2,0:T(8,128)(2,1)} %param.12) | copy-start | bytes 3145732
  227.7 0.6 copy-start.14
  231.0 2.0 copy-start
  233.0 4.2 copy-start.10
  233.9 6.6 copy-start.18
  238.6 5.6 copy-start.4
  240.5 1.9 copy-start.1
  243.3 0.8 copy-start.19
  244.1 3.1 copy-start.9
  244.1 3.1 copy-start.11
  250.5 1.9 copy-start.2
  253.4 0.8 copy-start.21
  254.2 3.1 copy-start.8
  254.2 3.1 copy-start.12
  260.5 1.9 copy-start.3
  263.6 0.8 copy-start.23
  264.4 3.1 copy-start.7
  264.4 3.1 copy-start.13
  269.0 4.8 copy-start.20
  269.0 4.8 copy-start.25
  273.8 4.8 copy-start.22
  273.8 4.8 copy-start.26
  278.6 4.8 copy-start.24
  278.6 4.8 copy-start.27
  288.3 3.7 copy-start.15
  288.3 3.7 copy-start.28
  288.3 3.7 copy-start.29
  288.3 3.7 copy-start.30
  294.1 434.0 %all-reduce.7.cloned.1.call-start = ((), (), s32[]{:S(2)}) async-start(), calls=%async_computation.3 | async-start | bytes 3145728 | tf_op jit(solution)/shard_map/psum | solution.py:114
Sparse Core Ops, SparseCore 0:
  10.1 77.2 all-gather.3
  89.5 70.0 all-gather.5
  294.3 272.7 all-reduce.4
  570.2 157.9 all-reduce.6
